TPU v7x, 32 devices: a whole 2x2x4 slice. The times are simulated.
32 devices in a mesh: bunch: 4 (over y, x), mp: 8 (over z, core).
Axes of the slice: x: 2, y: 2, z: 4, core: 2. Of those that a mesh axis runs over, the one named last changes fastest.
Arguments:
- phase_space: float32 [4, 64, 32768], P(None, 'bunch', 'mp')
- phase_advance: float32 [2, 64], P(None, 'bunch'), may hold values from 0.3 to 2.8
- centroid_history: float32 [2, 64, 64], P(None, None, 'bunch'), may hold values from -6 to 6
- lr_wake: float32 [4160], replicated, may hold values from -0.09375 to 0.09375
- sr_dipole: float32 [256, 256], replicated, may hold values from -24 to 24
- sr_quad: float32 [256, 256], replicated, may hold values from -24 to 24
- slice_ids: int32 [2, 64, 32768], P(None, 'bunch', 'mp'), may hold values from 0 to 255
Outputs:
- tracked: float32 [4, 64, 32768], P(None, 'bunch', 'mp')
- centroids: float32 [2, 2, 64], P(None, None, 'bunch')
All inputs are finite; a program needn't handle non-finite values.
Results may differ from a plain program's by a relative error of at most 0.00019.
Values sent between devices are 32-bit elements; how exact they have to be, the bound alone decides.
No kernel may reach another device: no remote copies, remote signals or barrier semaphores. Data moves between devices by JAX's collectives and lax.ppermute only.
A program may use at most 64 MiB of HBM per device.

v0:
```python
import jax
import jax.numpy as jnp
from jax import lax
from jax.sharding import PartitionSpec as P

SLICES = 256
TURNS = 2
DETUNE = 0.02


def body(phase_space, phase_advance, centroid_history, lr_wake, sr_dipole, sr_quad, slice_ids):
    highest = lax.Precision.HIGHEST
    bunch_dev = phase_space.shape[1]
    depth = centroid_history.shape[1]
    macro_total = phase_space.shape[2] * lax.axis_size("mp")
    all_bunches = bunch_dev * lax.axis_size("bunch")
    length = (depth + 1) * all_bunches
    offset_bunch = lax.axis_index("bunch") * bunch_dev
    own_index = jnp.arange(bunch_dev, dtype=jnp.int32)
    levels = jnp.arange(SLICES, dtype=jnp.int32)
    padded = jnp.concatenate([jnp.zeros((all_bunches,), jnp.float32), lr_wake])
    windows = jax.vmap(lambda start_at: lax.dynamic_slice(padded, (start_at,), (length,)))(
        offset_bunch + own_index
    )
    history = centroid_history
    whole = lax.all_gather(centroid_history, "bunch", axis=2, tiled=True)

    def moments_of(member):
        slice_line, line_x, line_y = member
        onehot = (slice_line[:, None] == levels[None, :]).astype(jnp.float32)
        stacked = jnp.stack([jnp.ones_like(line_x), line_x, line_y])
        return jnp.dot(stacked, onehot, precision=highest, preferred_element_type=jnp.float32)

    def lookup(member):
        slice_line, kick_rows = member
        onehot = (slice_line[:, None] == levels[None, :]).astype(jnp.float32)
        return lax.dot_general(
            kick_rows,
            onehot,
            (((1,), (1,)), ((), ())),
            precision=highest,
            preferred_element_type=jnp.float32,
        )

    coords = phase_space
    centroid_rows = []
    for turn_index in range(TURNS):
        slice_row = slice_ids[turn_index]
        moments = lax.map(moments_of, (slice_row, coords[0], coords[2]))
        moments = lax.psum(moments, "mp")
        density = moments[:, 0] / macro_total
        dipole = jnp.stack([moments[:, 1], moments[:, 2]]) / macro_total
        centroid = jnp.sum(dipole, axis=2)
        centroid_rows.append(centroid)
        dip_kick = jnp.einsum("pbj,ij->pbi", dipole, sr_dipole, precision=highest)
        quad_kick = jnp.einsum("bj,ij->bi", density, sr_quad, precision=highest)
        current_all = lax.all_gather(centroid, "bunch", axis=1, tiled=True)
        all_rows = jnp.concatenate([current_all[:, None, :], whole], axis=1)[:, :, ::-1].reshape(
            2, length
        )
        far_kick = jnp.einsum("bk,pk->pb", windows, all_rows, precision=highest)
        whole = jnp.concatenate([current_all[:, None, :], whole[:, :-1]], axis=1)
        kick_table = jnp.stack([dip_kick[0], dip_kick[1], quad_kick], axis=1)
        picked = lax.map(lookup, (slice_row, kick_table))
        coord_x, moment_x, coord_y, moment_y = (coords[0], coords[1], coords[2], coords[3])
        moment_x = moment_x + picked[:, 0] + picked[:, 2] * coord_x + far_kick[0][:, None]
        moment_y = moment_y + picked[:, 1] - picked[:, 2] * coord_y + far_kick[1][:, None]
        action = coord_x * coord_x + moment_x * moment_x + coord_y * coord_y + moment_y * moment_y
        angle_x = phase_advance[0][:, None] + DETUNE * action
        angle_y = phase_advance[1][:, None] + DETUNE * action
        new_x = jnp.cos(angle_x) * coord_x + jnp.sin(angle_x) * moment_x
        new_mx = -jnp.sin(angle_x) * coord_x + jnp.cos(angle_x) * moment_x
        new_y = jnp.cos(angle_y) * coord_y + jnp.sin(angle_y) * moment_y
        new_my = -jnp.sin(angle_y) * coord_y + jnp.cos(angle_y) * moment_y
        coords = jnp.stack([new_x, new_mx, new_y, new_my])
        history = jnp.concatenate([centroid[:, None, :], history[:, :-1]], axis=1)
    return (coords, jnp.stack(centroid_rows, axis=1))


def solution(mesh):
    placed = (
        P(None, "bunch", "mp"),
        P(None, "bunch"),
        P(None, None, "bunch"),
        P(),
        P(),
        P(),
        P(None, "bunch", "mp"),
    )
    return jax.shard_map(
        body,
        mesh=mesh,
        in_specs=placed,
        out_specs=(P(None, "bunch", "mp"), P(None, None, "bunch")),
        check_vma=False,
    )
```

profile of v0, /device:TPU:0, one launch (start us, length us, event | category | flops | bytes accessed | tf_op | source)
XLA Modules:
  0.0 306.1 jit_solution(7244623451006268379)
XLA Ops:
  1.6 9.9 %all_gather.10 = f32[2,64,64]{1,2,0:T(8,128)S(1)} all-gather(f32[2,64,16]{1,2,0:T(8,128)} %param.17), channel_id=1, replica_groups=mesh['bunch'=4,'mp'=8] {'bunch'}, dimensions={2}, use_global_device_ids=true | all-gather | bytes 40960 | tf_op jit(solution)/shard_map/all_gather | solution.py:26
  11.4 28.2 %while.45 = (s32[]{:T(128)}, f32[4224]{0:T(1024)S(1)}, s32[16,1]{0,1:T(1,128)S(1)}, f32[16,4160]{1,0:T(8,128)S(1)}, s32[]{:T(128)}, /*index=5*/s32[]{:T(128)}) while((s32[]{:T(128)}, f32[4224]{0:T(1024)S(1)}, s32[16,1]{0,1:T(1,128)S(1)}, f32[16,4160]{1,0:T(8,128)S(1)}, s32[]{:T(128)}, /*index=5*/s32[]{:T(128)}) %tuple.122), condition=%wide.while_cond, body=%wide.while_body.sunk | while | flops 2 | bytes 99937 | solution.py:22
  41.5 25.6 %while.46 = (s32[]{:T(128)}, f32[16,3,256]{2,0,1:T(8,128)S(1)}, f32[16,4096]{1,0:T(8,128)S(1)}, f32[16,4096]{1,0:T(8,128)S(1)}, s32[16,4096]{1,0:T(8,128)S(1)}, ...) while((s32[]{:T(128)}, f32[16,3,256]{2,0,1:T(8,128)S(1)}, f32[16,4096]{1,0:T(8,128)S(1)}, ...), condition=%wide.region_1.2_spmd.clone, body=%wide.region_0.1_spmd.clone.sunk | while | flops 38821888 | bytes 162961 | solution.py:49
  67.1 27.5 %psum.14 = f32[16,3,256]{2,0,1:T(8,128)S(1)} all-reduce(f32[16,3,256]{2,0,1:T(8,128)S(1)} %get-tuple-element.120), channel_id=1, replica_groups=mesh['bunch'=4,'mp'=8] {'mp'}, use_global_device_ids=true, to_apply=%region_2.3 | all-reduce | flops 12288 | bytes 98304 | tf_op jit(solution)/shard_map/psum | solution.py:50
  95.5 7.7 %all-gather = f32[4,16,2]{1,2,0:T(2,128)S(1)} all-gather(f32[1,16,2]{1,2,0:T(2,128)S(1)} %bitcast.229), channel_id=1, replica_groups=mesh['bunch'=4,'mp'=8] {'bunch'}, dimensions={0}, use_global_device_ids=true | all-gather | bytes 640 | tf_op jit(solution)/shard_map/all_gather | solution.py:57
  104.2 42.7 %while.47 = (s32[]{:T(128)}, f32[16,3,4096]{2,0,1:T(8,128)S(1)}, f32[16,3,256]{2,0,1:T(8,128)S(1)}, s32[16,4096]{1,0:T(8,128)S(1)}, s32[]{:T(128)}, /*index=5*/s32[]{:T(128)}) while((s32[]{:T(128)}, f32[16,3,4096]{2,0,1:T(8,128)S(1)}, f32[16,3,256]{2,0,1:T(8,128)S(1)}, s32[16,4096]{1,0:T(8,128)S(1)}, s32[]{:T(128)}, ...), condition=%wide.region_4.5_spmd.clone, body=%wide.region_3.4_spmd.clone.sunk | while | flops 38797312 | bytes 304217 | solution.py:64
  104.3 2.1 convolution_bitcast_fusion.6
  107.0 2.1 convolution_bitcast_fusion.6
  109.6 2.1 convolution_bitcast_fusion.6
  112.3 2.1 convolution_bitcast_fusion.6
  115.0 2.1 convolution_bitcast_fusion.6
  117.6 2.1 convolution_bitcast_fusion.6
  120.3 2.1 convolution_bitcast_fusion.6
  123.0 2.1 convolution_bitcast_fusion.6
  125.7 2.1 convolution_bitcast_fusion.6
  128.3 2.1 convolution_bitcast_fusion.6
  131.0 2.1 convolution_bitcast_fusion.6
  133.7 2.1 convolution_bitcast_fusion.6
  136.3 2.1 convolution_bitcast_fusion.6
  139.0 2.1 convolution_bitcast_fusion.6
  141.7 2.1 convolution_bitcast_fusion.6
  144.3 2.1 convolution_bitcast_fusion.6
  147.0 3.1 %multiply_add_fusion.5 = (f32[16,4096]{1,0:T(8,128)}, f32[16,4096]{1,0:T(8,128)}) fusion(f32[16]{0:T(128)S(1)} %get-tuple-element.281, f32[16]{0:T(128)S(1)} %get-tuple-element.285, f32[16,3,4096]{2,0,1:T(8,128)S(1)} %get-tuple-element.121, f32[4,16,4096]{2,1,0:T(8,128)S(1)} %copy-done.1, f32[16]{0:T(128)S(1)} %get-tuple-element.286, ...), kind=kLoop, calls=%fused_computation.81 | loop fusion | flops 1572864 | bytes 2359552 | tf_op jit(solution)/shard_map/add | solution.py:73
  150.9 55.3 %while.48 = (s32[]{:T(128)}, f32[16,3,256]{2,0,1:T(8,128)S(1)}, f32[16,4096]{1,0:T(8,128)}, f32[16,4096]{1,0:T(8,128)}, s32[16,4096]{1,0:T(8,128)}, /*index=5*/s32[]{:T(128)}, f32[]{:T(128)}, f32[]{:T(128)}, s32[]{:T(128)}) while((s32[]{:T(128)}, f32[16,3,256]{2,0,1:T(8,128)S(1)}, f32[16,4096]{1,0:T(8,128)}, f32[16,4096]{1,0:T(8,128)}, ...), condition=%wide.region_7.8_spmd.clone, body=%wide.region_6.7_spmd.clone.sunk | while | flops 38821888 | bytes 162961 | solution.py:49
  206.3 26.3 %psum.15 = f32[16,3,256]{2,0,1:T(8,128)S(1)} all-reduce(f32[16,3,256]{2,0,1:T(8,128)S(1)} %get-tuple-element.122), channel_id=1, replica_groups=mesh['bunch'=4,'mp'=8] {'mp'}, use_global_device_ids=true, to_apply=%region_8.9 | all-reduce | flops 12288 | bytes 98304 | tf_op jit(solution)/shard_map/psum | solution.py:50
  234.0 7.5 %all-gather.1 = f32[4,16,2]{1,2,0:T(2,128)S(1)} all-gather(f32[1,16,2]{1,2,0:T(2,128)S(1)} %bitcast.232), channel_id=1, replica_groups=mesh['bunch'=4,'mp'=8] {'bunch'}, dimensions={0}, use_global_device_ids=true | all-gather | bytes 640 | tf_op jit(solution)/shard_map/all_gather | solution.py:57
  242.5 57.1 %while.49 = (s32[]{:T(128)}, f32[16,3,4096]{2,0,1:T(8,128)S(1)}, f32[16,3,256]{2,0,1:T(8,128)S(1)}, s32[16,4096]{1,0:T(8,128)}, s32[]{:T(128)}, /*index=5*/s32[]{:T(128)}) while((s32[]{:T(128)}, f32[16,3,4096]{2,0,1:T(8,128)S(1)}, f32[16,3,256]{2,0,1:T(8,128)S(1)}, s32[16,4096]{1,0:T(8,128)}, s32[]{:T(128)}, ...), condition=%wide.region_10.11_spmd.clone, body=%wide.region_9.10_spmd.clone.sunk | while | flops 38797312 | bytes 304217 | solution.py:64
  243.5 2.1 convolution_bitcast_fusion.7
  254.2 2.1 convolution_bitcast_fusion.7
  257.8 2.1 convolution_bitcast_fusion.7
  299.6 3.3 %multiply_add_fusion.3 = (f32[1,16,4096]{2,1,0:T(8,128)S(1)}, f32[1,16,4096]{2,1,0:T(8,128)S(1)}, f32[1,16,4096]{2,1,0:T(8,128)S(1)}, f32[1,16,4096]{2,1,0:T(8,128)S(1)}, f32[1,16,4096]{2,1,0:T(8,128)S(1)}) fusion(f32[16]{0:T(128)S(1)} %copy-done.4, f32[16]{0:T(128)S(1)} %get-tuple-element.280, f32[16,3,4096]{2,0,1:T(8,128)S(1)} %get-tuple-element.123, ...), kind=kLoop, calls=%fused_computation.77 | loop fusion | flops 2359296 | bytes 3408128 | tf_op jit(solution)/shard_map/add | solution.py:71
  302.9 2.2 multiply_add_fusion.1
  (456 shorter events, 174.1 us)
Async XLA Ops:
  0.6 94.5 %copy-start = (f32[256,256]{1,0:T(8,128)S(1)}, f32[256,256]{1,0:T(8,128)}, u32[]{:S(2)}) copy-start(f32[256,256]{1,0:T(8,128)} %param.19) | copy-start | bytes 786436
  0.6 40.8 %copy-start.1 = (f32[4,16,4096]{2,1,0:T(8,128)S(1)}, f32[4,16,4096]{2,1,0:T(8,128)}, u32[]{:S(2)}) copy-start(f32[4,16,4096]{2,1,0:T(8,128)} %param.15) | copy-start | bytes 3145732
  41.5 53.2 %copy-start.2 = (f32[256,256]{1,0:T(8,128)S(1)}, f32[256,256]{1,0:T(8,128)}, u32[]{:S(2)}) copy-start(f32[256,256]{1,0:T(8,128)} %param.20) | copy-start | bytes 786436
  67.1 37.0 %copy-start.7 = (f32[2,16]{1,0:T(2,128)S(1)}, f32[2,16]{1,0:T(2,128)}, u32[]{:S(2)}) copy-start(f32[2,16]{1,0:T(2,128)} %param.16) | copy-start | bytes 388
  104.1 42.8 %copy-start.3 = (f32[16]{0:T(128)}, f32[16]{0:T(128)S(1)}, u32[]{:S(2)}) copy-start(f32[16]{0:T(128)S(1)} %get-tuple-element.282) | copy-start | bytes 196
  104.2 42.8 %copy-start.5 = (f32[16]{0:T(128)}, f32[16]{0:T(128)S(1)}, u32[]{:S(2)}) copy-start(f32[16]{0:T(128)S(1)} %get-tuple-element.285) | copy-start | bytes 196
  104.2 42.8 %copy-start.6 = (f32[16]{0:T(128)}, f32[16]{0:T(128)S(1)}, u32[]{:S(2)}) copy-start(f32[16]{0:T(128)S(1)} %get-tuple-element.286) | copy-start | bytes 196
  242.5 57.1 %copy-start.4 = (f32[16]{0:T(128)S(1)}, f32[16]{0:T(128)}, u32[]{:S(2)}) copy-start(f32[16]{0:T(128)} %copy-done.3) | copy-start | bytes 196
where the time goes:
time: 307 us; the launch traced here: 306 us
  matrix products  116 us (38%)
  local copies, waits for them, and re-layouts  95.8 us (31%)
  blocking collectives  78.9 us (26%)
  other arithmetic  10.8 us (4%)
  loops' own time  3.22 us (1%)
    dot_general x32, matrix products, lookup(): lax.dot_general(kick_rows, onehot, (((1,), (1,)), ((), ())), precision=hi...  68 us
    psum x2, blocking collectives, body(): moments = lax.psum(moments, 'mp')  53.9 us
    dynamic_slice x96, local copies, waits for them, and re-layouts, body(): moments = lax.map(moments_of, (slice_row, coords[0], coords[2]))  46.8 us
    dot_general x32, matrix products, moments_of(): jnp.dot(stacked, onehot, precision=highest, preferred_element_type=jnp.fl...  46.3 us
    gather x64, local copies, waits for them, and re-layouts  27.8 us
    all_gather x2, blocking collectives, body(): current_all = lax.all_gather(centroid, 'bunch', axis=1, tiled=True)  15.2 us
    dynamic_update_slice x64, local copies, waits for them, and re-layouts, body(): picked = lax.map(lookup, (slice_row, kick_table))  14.9 us
    all_gather x1, blocking collectives, body(): whole = lax.all_gather(centroid_history, 'bunch', axis=2, tiled=True)  9.87 us

commit v1 on v0

--- a/solution.py
+++ b/solution.py
@@ -47,7 +47,7 @@
     for turn_index in range(TURNS):
         slice_row = slice_ids[turn_index]
         moments = lax.map(moments_of, (slice_row, coords[0], coords[2]))
-        moments = lax.psum(moments, "mp")
+        moments = jnp.sum(lax.all_gather(moments, "mp"), axis=0)
         density = moments[:, 0] / macro_total
         dipole = jnp.stack([moments[:, 1], moments[:, 2]]) / macro_total
         centroid = jnp.sum(dipole, axis=2)

time: 307 us -> 283 us (0.922)
  blocking collectives: 78.9 us -> 54.7 us
    psum x2 -> x0, blocking collectives: 53.9 us -> none  [body(): moments = lax.psum(moments, 'mp')]
    all_gather x0 -> x2, blocking collectives: none -> 29.5 us  [body(): moments = jnp.sum(lax.all_gather(moments, 'mp'), axis=0)]
where the time goes in v1:
time: 283 us; the launch traced here: 282 us
  matrix products  116 us (41%)
  local copies, waits for them, and re-layouts  95.8 us (34%)
  blocking collectives  54.7 us (19%)
  other arithmetic  11 us (4%)
  loops' own time  3.22 us (1%)
    dot_general x32, matrix products, lookup(): lax.dot_general(kick_rows, onehot, (((1,), (1,)), ((), ())), precision=hi...  68 us
    dynamic_slice x96, local copies, waits for them, and re-layouts, body(): moments = lax.map(moments_of, (slice_row, coords[0], coords[2]))  46.8 us
    dot_general x32, matrix products, moments_of(): jnp.dot(stacked, onehot, precision=highest, preferred_element_type=jnp.fl...  46.3 us
    all_gather x2, blocking collectives, body(): moments = jnp.sum(lax.all_gather(moments, 'mp'), axis=0)  29.5 us
    gather x64, local copies, waits for them, and re-layouts  27.8 us
    all_gather x2, blocking collectives, body(): current_all = lax.all_gather(centroid, 'bunch', axis=1, tiled=True)  15.3 us
    dynamic_update_slice x64, local copies, waits for them, and re-layouts, body(): picked = lax.map(lookup, (slice_row, kick_table))  14.9 us
    all_gather x1, blocking collectives, body(): whole = lax.all_gather(centroid_history, 'bunch', axis=2, tiled=True)  9.87 us

profile of v1, /device:TPU:0, one launch (start us, length us, event | category | flops | bytes accessed | tf_op | source)
XLA Modules:
  0.0 282.0 jit_solution(17117864673506331025)
XLA Ops:
  1.6 9.9 %all_gather.24 = f32[2,64,64]{1,2,0:T(8,128)S(1)} all-gather(f32[2,64,16]{1,2,0:T(8,128)} %param.17), channel_id=1, replica_groups=mesh['bunch'=4,'mp'=8] {'bunch'}, dimensions={2}, use_global_device_ids=true | all-gather | bytes 40960 | tf_op jit(solution)/shard_map/all_gather | solution.py:26
  11.4 28.2 %while.45 = (s32[]{:T(128)}, f32[4224]{0:T(1024)S(1)}, s32[16,1]{0,1:T(1,128)S(1)}, f32[16,4160]{1,0:T(8,128)S(1)}, s32[]{:T(128)}, /*index=5*/s32[]{:T(128)}) while((s32[]{:T(128)}, f32[4224]{0:T(1024)S(1)}, s32[16,1]{0,1:T(1,128)S(1)}, f32[16,4160]{1,0:T(8,128)S(1)}, s32[]{:T(128)}, /*index=5*/s32[]{:T(128)}) %tuple.124), condition=%wide.while_cond, body=%wide.while_body.sunk | while | flops 2 | bytes 99937 | solution.py:22
  41.5 25.6 %while.46 = (s32[]{:T(128)}, f32[16,3,256]{2,0,1:T(8,128)S(1)}, f32[16,4096]{1,0:T(8,128)S(1)}, f32[16,4096]{1,0:T(8,128)S(1)}, s32[16,4096]{1,0:T(8,128)S(1)}, ...) while((s32[]{:T(128)}, f32[16,3,256]{2,0,1:T(8,128)S(1)}, f32[16,4096]{1,0:T(8,128)S(1)}, ...), condition=%wide.region_1.2_spmd.clone, body=%wide.region_0.1_spmd.clone.sunk | while | flops 38821888 | bytes 162961 | solution.py:49
  67.1 15.0 %all-gather = f32[128,3,256]{2,0,1:T(8,128)S(1)} all-gather(f32[16,3,256]{2,0,1:T(8,128)S(1)} %get-tuple-element.120), channel_id=2, replica_groups=mesh['bunch'=4,'mp'=8] {'mp'}, dimensions={0}, use_global_device_ids=true | all-gather | bytes 442368 | tf_op jit(solution)/shard_map/all_gather | solution.py:50
  83.0 7.9 %all-gather.2 = f32[4,16,2]{1,2,0:T(2,128)S(1)} all-gather(f32[1,16,2]{1,2,0:T(2,128)S(1)} %bitcast.233), channel_id=1, replica_groups=mesh['bunch'=4,'mp'=8] {'bunch'}, dimensions={0}, use_global_device_ids=true | all-gather | bytes 640 | tf_op jit(solution)/shard_map/all_gather | solution.py:57
  92.0 42.7 %while.47 = (s32[]{:T(128)}, f32[16,3,4096]{2,0,1:T(8,128)S(1)}, f32[16,3,256]{2,0,1:T(8,128)S(1)}, s32[16,4096]{1,0:T(8,128)S(1)}, s32[]{:T(128)}, /*index=5*/s32[]{:T(128)}) while((s32[]{:T(128)}, f32[16,3,4096]{2,0,1:T(8,128)S(1)}, f32[16,3,256]{2,0,1:T(8,128)S(1)}, s32[16,4096]{1,0:T(8,128)S(1)}, s32[]{:T(128)}, ...), condition=%wide.region_4.5_spmd.clone, body=%wide.region_3.4_spmd.clone.sunk | while | flops 38797312 | bytes 304217 | solution.py:64
  92.0 2.1 convolution_bitcast_fusion.6
  94.7 2.1 convolution_bitcast_fusion.6
  97.4 2.1 convolution_bitcast_fusion.6
  100.0 2.1 convolution_bitcast_fusion.6
  102.7 2.1 convolution_bitcast_fusion.6
  105.4 2.1 convolution_bitcast_fusion.6
  108.0 2.1 convolution_bitcast_fusion.6
  110.7 2.1 convolution_bitcast_fusion.6
  113.4 2.1 convolution_bitcast_fusion.6
  116.1 2.1 convolution_bitcast_fusion.6
  118.7 2.1 convolution_bitcast_fusion.6
  134.7 3.1 %multiply_add_fusion.5 = (f32[16,4096]{1,0:T(8,128)}, f32[16,4096]{1,0:T(8,128)}) fusion(f32[16]{0:T(128)S(1)} %get-tuple-element.283, f32[16]{0:T(128)S(1)} %get-tuple-element.287, f32[16,3,4096]{2,0,1:T(8,128)S(1)} %get-tuple-element.121, f32[4,16,4096]{2,1,0:T(8,128)S(1)} %copy-done.1, f32[16]{0:T(128)S(1)} %get-tuple-element.288, ...), kind=kLoop, calls=%fused_computation.81 | loop fusion | flops 1572864 | bytes 2359552 | tf_op jit(solution)/shard_map/add | solution.py:73
  138.7 55.3 %while.48 = (s32[]{:T(128)}, f32[16,3,256]{2,0,1:T(8,128)S(1)}, f32[16,4096]{1,0:T(8,128)}, f32[16,4096]{1,0:T(8,128)}, s32[16,4096]{1,0:T(8,128)}, /*index=5*/s32[]{:T(128)}, f32[]{:T(128)}, f32[]{:T(128)}, s32[]{:T(128)}) while((s32[]{:T(128)}, f32[16,3,256]{2,0,1:T(8,128)S(1)}, f32[16,4096]{1,0:T(8,128)}, f32[16,4096]{1,0:T(8,128)}, ...), condition=%wide.region_7.8_spmd.clone, body=%wide.region_6.7_spmd.clone.sunk | while | flops 38821888 | bytes 162961 | solution.py:49
  194.0 14.5 %all-gather.1 = f32[128,3,256]{2,0,1:T(8,128)S(1)} all-gather(f32[16,3,256]{2,0,1:T(8,128)S(1)} %get-tuple-element.122), channel_id=3, replica_groups=mesh['bunch'=4,'mp'=8] {'mp'}, dimensions={0}, use_global_device_ids=true | all-gather | bytes 442368 | tf_op jit(solution)/shard_map/all_gather | solution.py:50
  210.0 7.4 %all-gather.3 = f32[4,16,2]{1,2,0:T(2,128)S(1)} all-gather(f32[1,16,2]{1,2,0:T(2,128)S(1)} %bitcast.236), channel_id=1, replica_groups=mesh['bunch'=4,'mp'=8] {'bunch'}, dimensions={0}, use_global_device_ids=true | all-gather | bytes 640 | tf_op jit(solution)/shard_map/all_gather | solution.py:57
  218.4 57.1 %while.49 = (s32[]{:T(128)}, f32[16,3,4096]{2,0,1:T(8,128)S(1)}, f32[16,3,256]{2,0,1:T(8,128)S(1)}, s32[16,4096]{1,0:T(8,128)}, s32[]{:T(128)}, /*index=5*/s32[]{:T(128)}) while((s32[]{:T(128)}, f32[16,3,4096]{2,0,1:T(8,128)S(1)}, f32[16,3,256]{2,0,1:T(8,128)S(1)}, s32[16,4096]{1,0:T(8,128)}, s32[]{:T(128)}, ...), condition=%wide.region_10.11_spmd.clone, body=%wide.region_9.10_spmd.clone.sunk | while | flops 38797312 | bytes 304217 | solution.py:64
  219.4 2.1 convolution_bitcast_fusion.7
  230.1 2.1 convolution_bitcast_fusion.7
  240.8 2.1 convolution_bitcast_fusion.7
  244.4 2.1 convolution_bitcast_fusion.7
  255.1 2.1 convolution_bitcast_fusion.7
  258.6 2.1 convolution_bitcast_fusion.7
  269.4 2.1 convolution_bitcast_fusion.7
  272.9 2.1 convolution_bitcast_fusion.7
  275.5 3.3 %multiply_add_fusion.3 = (f32[1,16,4096]{2,1,0:T(8,128)S(1)}, f32[1,16,4096]{2,1,0:T(8,128)S(1)}, f32[1,16,4096]{2,1,0:T(8,128)S(1)}, f32[1,16,4096]{2,1,0:T(8,128)S(1)}, f32[1,16,4096]{2,1,0:T(8,128)S(1)}) fusion(f32[16]{0:T(128)S(1)} %copy-done.4, f32[16]{0:T(128)S(1)} %get-tuple-element.282, f32[16,3,4096]{2,0,1:T(8,128)S(1)} %get-tuple-element.123, ...), kind=kLoop, calls=%fused_computation.77 | loop fusion | flops 2359296 | bytes 3408128 | tf_op jit(solution)/shard_map/add | solution.py:71
  278.8 2.2 multiply_add_fusion.1
  (460 shorter events, 174.2 us)
Async XLA Ops:
  0.6 82.0 %copy-start = (f32[256,256]{1,0:T(8,128)S(1)}, f32[256,256]{1,0:T(8,128)}, u32[]{:S(2)}) copy-start(f32[256,256]{1,0:T(8,128)} %param.19) | copy-start | bytes 786436
  0.6 40.8 %copy-start.1 = (f32[4,16,4096]{2,1,0:T(8,128)S(1)}, f32[4,16,4096]{2,1,0:T(8,128)}, u32[]{:S(2)}) copy-start(f32[4,16,4096]{2,1,0:T(8,128)} %param.15) | copy-start | bytes 3145732
  67.1 15.1 %copy-start.2 = (f32[256,256]{1,0:T(8,128)S(1)}, f32[256,256]{1,0:T(8,128)}, u32[]{:S(2)}) copy-start(f32[256,256]{1,0:T(8,128)} %param.20) | copy-start | bytes 786436
  82.2 9.7 %copy-start.7 = (f32[2,16]{1,0:T(2,128)S(1)}, f32[2,16]{1,0:T(2,128)}, u32[]{:S(2)}) copy-start(f32[2,16]{1,0:T(2,128)} %param.16) | copy-start | bytes 388
  91.9 42.8 %copy-start.3 = (f32[16]{0:T(128)}, f32[16]{0:T(128)S(1)}, u32[]{:S(2)}) copy-start(f32[16]{0:T(128)S(1)} %get-tuple-element.284) | copy-start | bytes 196
  91.9 42.8 %copy-start.5 = (f32[16]{0:T(128)}, f32[16]{0:T(128)S(1)}, u32[]{:S(2)}) copy-start(f32[16]{0:T(128)S(1)} %get-tuple-element.287) | copy-start | bytes 196
  91.9 42.8 %copy-start.6 = (f32[16]{0:T(128)}, f32[16]{0:T(128)S(1)}, u32[]{:S(2)}) copy-start(f32[16]{0:T(128)S(1)} %get-tuple-element.288) | copy-start | bytes 196
  218.4 57.1 %copy-start.4 = (f32[16]{0:T(128)S(1)}, f32[16]{0:T(128)}, u32[]{:S(2)}) copy-start(f32[16]{0:T(128)} %copy-done.3) | copy-start | bytes 196
